TPU v7x, 32 devices: a whole 2x2x4 slice. The times are simulated.
32 devices in a mesh: seq: 8 (over z, y), head: 4 (over x, core).
Axes of the slice: x: 2, y: 2, z: 4, core: 2. Of those that a mesh axis runs over, the one named last changes fastest.
Arguments:
- layer_input: bfloat16 [4096, 768], P('seq', 'head'), may hold values from -6 to 6
- ln1_gain: float32 [768], replicated, may hold values from 0.5 to 1.5
- ln1_bias: float32 [768], replicated, may hold values from -3 to 3
- w_query: bfloat16 [768, 768], P(None, 'head'), may hold values from -0.21875 to 0.21875
- b_query: float32 [768], P('head'), may hold values from -3 to 3
- w_key: bfloat16 [768, 768], P(None, 'head'), may hold values from -0.3125 to 0.3125
- w_value: bfloat16 [768, 768], P(None, 'head'), may hold values from -0.21875 to 0.21875
- b_value: float32 [768], P('head'), may hold values from -1.2 to 1.2
- sub_gain: float32 [768], P('head'), may hold values from 0.5 to 1.5
- sub_bias: float32 [768], P('head'), may hold values from -3 to 3
- w_out: bfloat16 [768, 768], P('head'), may hold values from -0.21875 to 0.21875
- b_out: float32 [768], replicated, may hold values from -3 to 3
- ln2_gain: float32 [768], replicated, may hold values from 0.5 to 1.5
- ln2_bias: float32 [768], replicated, may hold values from -3 to 3
- w_up: bfloat16 [768, 3072], P(None, 'head'), may hold values from -0.21875 to 0.21875
- b_up: float32 [3072], P('head'), may hold values from -3 to 3
- w_down: bfloat16 [3072, 768], P('head'), may hold values from -0.109375 to 0.109375
- b_down: float32 [768], replicated, may hold values from -3 to 3
- cotangent: bfloat16 [4096, 768], P('seq', 'head'), may hold values from -6 to 6
- row_lengths: int32 [6], replicated, may hold values from 1 to 3072, 4096 in all
Outputs:
- layer_output: bfloat16 [4096, 768], P('seq', 'head')
- grad_input: float32 [4096, 768], P('seq', 'head')
- grad_ln1_gain: float32 [768], replicated
- grad_ln1_bias: float32 [768], replicated
- grad_w_query: float32 [768, 768], P(None, 'head')
- grad_b_query: float32 [768], P('head')
- grad_w_key: float32 [768, 768], P(None, 'head')
- grad_w_value: float32 [768, 768], P(None, 'head')
- grad_b_value: float32 [768], P('head')
- grad_sub_gain: float32 [768], P('head')
- grad_sub_bias: float32 [768], P('head')
- grad_w_out: float32 [768, 768], P('head')
- grad_b_out: float32 [768], replicated
- grad_ln2_gain: float32 [768], replicated
- grad_ln2_bias: float32 [768], replicated
- grad_w_up: float32 [768, 3072], P(None, 'head')
- grad_b_up: float32 [3072], P('head')
- grad_w_down: float32 [3072, 768], P('head')
- grad_b_down: float32 [768], replicated
Inputs may be any that keep to these rules, and one draw needn't show every extreme that they name: `row_lengths`: the 6 row lengths sum to 4096, and the longest is exactly 3072.
All inputs are finite; a program needn't handle non-finite values.
Results may differ from a plain program's by a relative error of at most 0.018.
Values may be sent and summed in bfloat16 or wider, within the bound.
No kernel may reach another device: no remote copies, remote signals or barrier semaphores. Data moves between devices by JAX's collectives and lax.ppermute only.
A program may use at most 256 MiB of HBM per device.

v0:
```python
import math
import jax
import jax.numpy as jnp
from jax import lax
from jax.sharding import PartitionSpec as P

HEAD_DIM = 64
SEG = 2048
eps = 1e-05
segment_scales = (1, 2, 4, 8, 16)
dilation_steps = (1, 2, 4, 6, 12)


def layer_norm(inputs, norm_gain, norm_bias):
    center = inputs - jnp.mean(inputs, axis=-1, keepdims=True)
    spread = jnp.mean(center * center, axis=-1, keepdims=True)
    return center * lax.rsqrt(spread + eps) * norm_gain + norm_bias


def token_places(positions, lengths):
    row_ends = jnp.cumsum(lengths)
    starts = row_ends - lengths
    row_of = jnp.sum((positions[:, None] >= row_ends[None, :]).astype(jnp.int32), axis=1)
    onehot = (row_of[:, None] == jnp.arange(lengths.shape[0], dtype=jnp.int32)[None, :]).astype(
        jnp.int32
    )
    row_place = positions - jnp.sum(onehot * starts[None, :], axis=1)
    return (row_of, row_place)


def pattern_count(head_ids, query_row, query_place, key_row, key_place):
    allowed = (query_row[:, None] == key_row[None, :]) & (
        key_place[None, :] <= query_place[:, None]
    )
    counted = jnp.zeros((head_ids.shape[0], query_row.shape[0], key_row.shape[0]), jnp.float32)
    for scale_factor, step_size in zip(segment_scales, dilation_steps):
        seg_width = SEG * scale_factor
        same_seg = allowed & (query_place[:, None] // seg_width == key_place[None, :] // seg_width)
        offset = head_ids % step_size
        query_on = (query_place % seg_width % step_size)[None, :] == offset[:, None]
        key_on = (key_place % seg_width % step_size)[None, :] == offset[:, None]
        counted = counted + (same_seg[None] & query_on[:, :, None] & key_on[:, None, :]).astype(
            jnp.float32
        )
    return counted


def fold_keys(running, pieces, queries, head_ids, query_row, query_place, lengths, score_scale):
    key_rows, values = pieces
    piece_rows = key_rows.shape[0]
    block_rows = math.gcd(piece_rows, 2048)
    local_heads = queries.shape[0]
    key_blocks = key_rows.reshape(piece_rows // block_rows, block_rows, local_heads, -1)
    value_blocks = values.reshape(piece_rows // block_rows, block_rows, local_heads, -1)
    offsets = jnp.arange(piece_rows // block_rows, dtype=jnp.int32) * block_rows

    def advance(status, element):
        highest, totals, running_sum = status
        key_blk, value_blk, block_first = element
        key_row, key_place = token_places(
            block_first + jnp.arange(block_rows, dtype=jnp.int32), lengths
        )
        counted = pattern_count(head_ids, query_row, query_place, key_row, key_place)
        scores = (
            jnp.einsum("hqd,khd->hqk", queries, key_blk, preferred_element_type=jnp.float32)
            * score_scale
        )
        masked = jnp.where(counted > 0, scores, -1e30)
        new_high = jnp.maximum(highest, jnp.max(masked, axis=-1))
        weights = counted * jnp.exp(masked - new_high[..., None])
        factor = jnp.exp(highest - new_high)
        totals = totals * factor + jnp.sum(weights, axis=-1)
        running_sum = running_sum * factor[..., None] + jnp.einsum(
            "hqk,khd->hqd",
            weights.astype(jnp.bfloat16),
            value_blk,
            preferred_element_type=jnp.float32,
        )
        return ((new_high, totals, running_sum), None)

    running, unused = lax.scan(advance, running, (key_blocks, value_blocks, offsets))
    return running


def shards(
    layer_input,
    ln1_gain,
    ln1_bias,
    w_query,
    b_query,
    w_key,
    w_value,
    b_value,
    sub_gain,
    sub_bias,
    w_out,
    b_out,
    ln2_gain,
    ln2_bias,
    w_up,
    b_up,
    w_down,
    b_down,
    cotangent,
    row_lengths,
):
    rows_local = layer_input.shape[0]
    slice_width = layer_input.shape[1]
    head_share = w_query.shape[1]
    local_heads = head_share // HEAD_DIM
    head_pos = lax.axis_index("head")
    seq_pos = lax.axis_index("seq")
    full_width = head_share * lax.axis_size("head")
    score_scale = HEAD_DIM ** (-0.5)
    head_ids = head_pos * local_heads + jnp.arange(local_heads, dtype=jnp.int32)
    own_index = seq_pos * rows_local + jnp.arange(rows_local, dtype=jnp.int32)
    query_row, query_place = token_places(own_index, row_lengths)
    input_whole = lax.all_gather(layer_input, "head", axis=1, tiled=True).astype(jnp.float32)
    normed = layer_norm(input_whole, ln1_gain, ln1_bias).astype(jnp.bfloat16)
    queries = (jnp.dot(normed, w_query, preferred_element_type=jnp.float32) + b_query).astype(
        jnp.bfloat16
    )
    key_rows = jnp.dot(normed, w_key, preferred_element_type=jnp.float32).astype(jnp.bfloat16)
    values = (jnp.dot(normed, w_value, preferred_element_type=jnp.float32) + b_value).astype(
        jnp.bfloat16
    )
    query_heads = queries.reshape(rows_local, local_heads, HEAD_DIM).transpose(1, 0, 2)
    start_state = (
        jnp.full((local_heads, rows_local), -1e30, jnp.float32),
        jnp.zeros((local_heads, rows_local), jnp.float32),
        jnp.zeros((local_heads, rows_local, HEAD_DIM), jnp.float32),
    )
    highest, totals, running_sum = fold_keys(
        start_state,
        (
            lax.all_gather(key_rows, "seq", axis=0, tiled=True),
            lax.all_gather(values, "seq", axis=0, tiled=True),
        ),
        query_heads,
        head_ids,
        query_row,
        query_place,
        row_lengths,
        score_scale,
    )
    attended = running_sum / totals[..., None]
    log_total = highest + jnp.log(totals)
    mixed_heads = attended.transpose(1, 0, 2).reshape(rows_local, head_share)
    row_sum, row_square = lax.psum(
        (jnp.sum(mixed_heads, axis=1), jnp.sum(mixed_heads * mixed_heads, axis=1)), "head"
    )
    mean_value = row_sum / full_width
    inv_std = lax.rsqrt(row_square / full_width - mean_value * mean_value + eps)
    centered = (mixed_heads - mean_value[:, None]) * inv_std[:, None]
    sub_out = (centered * sub_gain + sub_bias).astype(jnp.bfloat16)
    projected = lax.psum_scatter(
        jnp.dot(sub_out, w_out, preferred_element_type=jnp.float32).astype(jnp.bfloat16),
        "head",
        scatter_dimension=1,
        tiled=True,
    ).astype(jnp.float32)
    out_bias_share = lax.dynamic_slice_in_dim(b_out, head_pos * slice_width, slice_width, 0)
    middle = layer_input.astype(jnp.float32) + (projected + out_bias_share)
    middle_whole = lax.all_gather(middle.astype(jnp.bfloat16), "head", axis=1, tiled=True).astype(
        middle.dtype
    )
    normed_mid = layer_norm(middle_whole, ln2_gain, ln2_bias).astype(jnp.bfloat16)
    inner_act = jnp.dot(normed_mid, w_up, preferred_element_type=jnp.float32) + b_up
    active = jax.nn.gelu(inner_act, approximate=False).astype(jnp.bfloat16)
    ffn_out = lax.psum_scatter(
        jnp.dot(active, w_down, preferred_element_type=jnp.float32).astype(jnp.bfloat16),
        "head",
        scatter_dimension=1,
        tiled=True,
    ).astype(jnp.float32)
    down_bias_share = lax.dynamic_slice_in_dim(b_down, head_pos * slice_width, slice_width, 0)
    layer_output = (middle + (ffn_out + down_bias_share)).astype(jnp.bfloat16)
    grad_whole = lax.all_gather(cotangent, "head", axis=1, tiled=True)
    grad_float = grad_whole.astype(jnp.float32)
    grad_w_down = jnp.dot(active.T, grad_whole, preferred_element_type=jnp.float32)
    grad_b_down = jnp.sum(grad_float, axis=0)
    grad_active = jnp.dot(grad_whole, w_down.T, preferred_element_type=jnp.float32)
    unused, gelu_back = jax.vjp(lambda inputs: jax.nn.gelu(inputs, approximate=False), inner_act)
    grad_inner = gelu_back(grad_active)[0].astype(jnp.bfloat16)
    grad_w_up = jnp.dot(normed_mid.T, grad_inner, preferred_element_type=jnp.float32)
    grad_b_up = jnp.sum(grad_inner.astype(jnp.float32), axis=0)
    grad_norm_mid = lax.psum(
        jnp.dot(grad_inner, w_up.T, preferred_element_type=jnp.float32).astype(jnp.bfloat16), "head"
    ).astype(jnp.float32)
    unused, mid_back = jax.vjp(layer_norm, middle_whole, ln2_gain, ln2_bias)
    grad_mid_norm, grad_ln2_gain, grad_ln2_bias = mid_back(grad_norm_mid)
    grad_middle = grad_float + grad_mid_norm
    grad_branch = grad_middle.astype(jnp.bfloat16)
    grad_b_out = jnp.sum(grad_branch.astype(jnp.float32), axis=0)
    grad_w_out = jnp.dot(sub_out.T, grad_branch, preferred_element_type=jnp.float32)
    grad_sub = jnp.dot(grad_branch, w_out.T, preferred_element_type=jnp.float32)
    grad_sub_gain = jnp.sum(grad_sub * centered, axis=0)
    grad_sub_bias = jnp.sum(grad_sub, axis=0)
    grad_hat = grad_sub * sub_gain
    hat_sum, hat_cross = lax.psum(
        (jnp.sum(grad_hat, axis=1), jnp.sum(grad_hat * centered, axis=1)), "head"
    )
    grad_mixed = inv_std[:, None] * (
        grad_hat - hat_sum[:, None] / full_width - centered * hat_cross[:, None] / full_width
    )
    grad_heads = (
        grad_mixed.reshape(rows_local, local_heads, HEAD_DIM)
        .transpose(1, 0, 2)
        .astype(jnp.bfloat16)
    )
    dot_term = jnp.sum(grad_heads.astype(jnp.float32) * attended, axis=-1)
    key_all, value_all = (
        lax.all_gather(key_rows, "seq", axis=0, tiled=True),
        lax.all_gather(values, "seq", axis=0, tiled=True),
    )
    total_rows = key_all.shape[0]
    block_rows = math.gcd(total_rows, 2048)
    key_blocks = key_all.reshape(total_rows // block_rows, block_rows, local_heads, HEAD_DIM)
    value_blocks = value_all.reshape(total_rows // block_rows, block_rows, local_heads, HEAD_DIM)
    offsets = jnp.arange(total_rows // block_rows, dtype=jnp.int32) * block_rows

    def score_parts(
        query_blk, grad_blk, log_blk, dot_blk, q_row, q_place, key_blk, value_blk, k_row, k_place
    ):
        counted = pattern_count(head_ids, q_row, q_place, k_row, k_place)
        scores = (
            jnp.einsum("hqd,khd->hqk", query_blk, key_blk, preferred_element_type=jnp.float32)
            * score_scale
        )
        masked = jnp.where(counted > 0, scores, -1e30)
        weights_norm = counted * jnp.exp(masked - log_blk[..., None])
        grad_probs = jnp.einsum(
            "hqd,khd->hqk", grad_blk, value_blk, preferred_element_type=jnp.float32
        )
        grad_scores = (weights_norm * (grad_probs - dot_blk[..., None])).astype(jnp.bfloat16)
        return (weights_norm, grad_scores)

    def back_step(grad_query_sum, element):
        key_blk, value_blk, block_first = element
        key_row, key_place = token_places(
            block_first + jnp.arange(block_rows, dtype=jnp.int32), row_lengths
        )
        weights_norm, grad_scores = score_parts(
            query_heads,
            grad_heads,
            log_total,
            dot_term,
            query_row,
            query_place,
            key_blk,
            value_blk,
            key_row,
            key_place,
        )
        grad_query_sum = grad_query_sum + jnp.einsum(
            "hqk,khd->hqd", grad_scores, key_blk, preferred_element_type=jnp.float32
        )
        grad_value = jnp.einsum(
            "hqk,hqd->khd",
            weights_norm.astype(jnp.bfloat16),
            grad_heads,
            preferred_element_type=jnp.float32,
        )
        grad_key = jnp.einsum(
            "hqk,hqd->khd", grad_scores, query_heads, preferred_element_type=jnp.float32
        )
        key_terms = jnp.concatenate(
            [grad_key.reshape(block_rows, -1) * score_scale, grad_value.reshape(block_rows, -1)],
            axis=1,
        )
        return (grad_query_sum, key_terms)

    query_zero = jnp.zeros((local_heads, rows_local, HEAD_DIM), jnp.float32)
    grad_query_sum, key_terms = lax.scan(back_step, query_zero, (key_blocks, value_blocks, offsets))
    key_terms = key_terms.reshape(total_rows, 2 * head_share)
    kv_grads = lax.psum_scatter(key_terms, "seq", scatter_dimension=0, tiled=True)
    grad_keys = kv_grads[:, :head_share].astype(jnp.bfloat16)
    grad_values = kv_grads[:, head_share:].astype(jnp.bfloat16)
    grad_queries = (grad_query_sum * score_scale).transpose(1, 0, 2).reshape(rows_local, head_share)
    grad_queries = grad_queries.astype(jnp.bfloat16)
    grad_w_query = jnp.dot(normed.T, grad_queries, preferred_element_type=jnp.float32)
    grad_b_query = jnp.sum(grad_queries.astype(jnp.float32), axis=0)
    grad_w_key = jnp.dot(normed.T, grad_keys, preferred_element_type=jnp.float32)
    grad_w_value = jnp.dot(normed.T, grad_values, preferred_element_type=jnp.float32)
    grad_b_value = jnp.sum(grad_values.astype(jnp.float32), axis=0)
    grad_normed = (
        jnp.dot(grad_queries, w_query.T, preferred_element_type=jnp.float32)
        + jnp.dot(grad_keys, w_key.T, preferred_element_type=jnp.float32)
        + jnp.dot(grad_values, w_value.T, preferred_element_type=jnp.float32)
    )
    grad_normed = lax.psum(grad_normed.astype(jnp.bfloat16), "head").astype(jnp.float32)
    unused, input_back = jax.vjp(layer_norm, input_whole, ln1_gain, ln1_bias)
    grad_in_norm, grad_ln1_gain, grad_ln1_bias = input_back(grad_normed)
    grad_input_whole = grad_middle + grad_in_norm
    grad_input = lax.dynamic_slice_in_dim(grad_input_whole, head_pos * slice_width, slice_width, 1)
    summed = lax.psum(
        (
            grad_ln1_gain,
            grad_ln1_bias,
            grad_w_query,
            grad_b_query,
            grad_w_key,
            grad_w_value,
            grad_b_value,
            grad_sub_gain,
            grad_sub_bias,
            grad_w_out,
            grad_b_out,
            grad_ln2_gain,
            grad_ln2_bias,
            grad_w_up,
            grad_b_up,
            grad_w_down,
            grad_b_down,
        ),
        "seq",
    )
    return (layer_output, grad_input) + tuple(summed)


def solution(mesh):
    in_specs = (
        P("seq", "head"),
        P(),
        P(),
        P(None, "head"),
        P("head"),
        P(None, "head"),
        P(None, "head"),
        P("head"),
        P("head"),
        P("head"),
        P("head", None),
        P(),
        P(),
        P(),
        P(None, "head"),
        P("head"),
        P("head", None),
        P(),
        P("seq", "head"),
        P(),
    )
    out_specs = (
        P("seq", "head"),
        P("seq", "head"),
        P(),
        P(),
        P(None, "head"),
        P("head"),
        P(None, "head"),
        P(None, "head"),
        P("head"),
        P("head"),
        P("head"),
        P("head", None),
        P(),
        P(),
        P(),
        P(None, "head"),
        P("head"),
        P("head", None),
        P(),
    )
    return jax.shard_map(shards, mesh=mesh, in_specs=in_specs, out_specs=out_specs, check_vma=False)
```

profile of v0, /device:TPU:0, one launch (start us, length us, event | category | flops | bytes accessed | tf_op | source)
XLA Modules:
  0.0 842.9 jit_solution(17732856070422200237)
XLA Ops:
  7.3 10.4 %all_gather.17 = bf16[512,768]{0,1:T(8,128)(2,1)S(1)} all-gather(bf16[512,192]{0,1:T(8,128)(2,1)} %param.24), channel_id=1, replica_groups=mesh['seq'=8,'head'=4] {'head'}, dimensions={1}, use_global_device_ids=true | all-gather | bytes 983040 | tf_op jit(solution)/shard_map/all_gather | solution.py:118
  22.7 43.9 %all-gather.3.cloned.1.call-done = bf16[4096,192]{0,1:T(8,128)(2,1)} async-done(((bf16[512,192]{0,1:T(8,128)(2,1)}), bf16[4096,192]{0,1:T(8,128)(2,1)}) %all-gather.3.cloned.1.call-update) | async-done | bytes 1572880 | tf_op jit(solution)/shard_map/all_gather | solution.py:136
  71.2 41.5 %all-gather.5.cloned.1.call-done = bf16[4096,192]{0,1:T(8,128)(2,1)} async-done(((bf16[512,192]{0,1:T(8,128)(2,1)}), bf16[4096,192]{0,1:T(8,128)(2,1)}) %all-gather.5.cloned.1.call-update) | async-done | bytes 1572880 | tf_op jit(solution)/shard_map/all_gather | solution.py:137
  117.4 77.7 %while.42 = (s32[]{:T(128)}, f32[3,512]{1,0:T(4,128)S(1)}, f32[3,512]{1,0:T(4,128)}, f32[3,512,64]{1,2,0:T(8,128)}, s32[512]{0:T(512)S(1)}, /*index=5*/s32[2]{0:...) while((s32[]{:T(128)}, f32[3,512]{1,0:T(4,128)S(1)}, ...), condition=%wide.region_10.11_spmd.clone.clone.clone, body=%wide.region_5.10_spmd.clone.clone.clone.sunk | while | flops 955956864 | bytes 106965376 | solution.py:81
  125.2 12.1 %fusion.202 = (f32[3,512]{1,0:T(4,128)S(1)}, f32[3,2048,512]{2,1,0:T(8,128)}) fusion(f32[512,2048]{0,1:T(8,128)S(1)} %get-tuple-element.1711, pred[3,2048]{1,0:T(4,128)(4,1)S(1)} %broadcast_compare_fusion.38, pred[3,512]{1,0:T(4,128)(4,1)S(1)} %broadcast_compare_fusion.39, pred[512,2048]{0,1:T(8,128)(4,1)S(1)} %get-tuple-element.1716, ...), kind=kOutput, calls=%fused_computation.7.clone.1 | convolution fusion | flops 465566208 | bytes 22001668 | tf_op jit(solution)/shard_map/while/body/eval_jaxpr/hqd,khd->hqk/dot_general | solution.py:65
  137.4 16.7 %fusion.203 = (f32[3,512]{1,0:T(4,128)S(1)}, bf16[3,512,2048]{1,2,0:T(8,128)(2,1)S(1)}) fusion(f32[3,512]{1,0:T(4,128)S(1)} %select_maximum_fusion.2, f32[3,2048,512]{2,1,0:T(8,128)} %get-tuple-element.1730, pred[3,2048]{1,0:T(4,128)(4,1)S(1)} %broadcast_compare_fusion.38, pred[3,512]{1,0:T(4,128)(4,1)S(1)} %broadcast_compare_fusion.39, ...), kind=kLoop, calls=%fused_computation.388.clone.1 | loop fusion | flops 72350208 | bytes 27305984 | tf_op jit(solution)/shard_map/while/body/eval_jaxpr/reduce_sum | solution.py:72
  164.1 12.1 %fusion.202 = (f32[3,512]{1,0:T(4,128)S(1)}, f32[3,2048,512]{2,1,0:T(8,128)}) fusion(f32[512,2048]{0,1:T(8,128)S(1)} %get-tuple-element.1711, pred[3,2048]{1,0:T(4,128)(4,1)S(1)} %broadcast_compare_fusion.38, pred[3,512]{1,0:T(4,128)(4,1)S(1)} %broadcast_compare_fusion.39, pred[512,2048]{0,1:T(8,128)(4,1)S(1)} %get-tuple-element.1716, ...), kind=kOutput, calls=%fused_computation.7.clone.1 | convolution fusion | flops 465566208 | bytes 22001668 | tf_op jit(solution)/shard_map/while/body/eval_jaxpr/hqd,khd->hqk/dot_general | solution.py:65
  176.3 16.7 %fusion.203 = (f32[3,512]{1,0:T(4,128)S(1)}, bf16[3,512,2048]{1,2,0:T(8,128)(2,1)S(1)}) fusion(f32[3,512]{1,0:T(4,128)S(1)} %select_maximum_fusion.2, f32[3,2048,512]{2,1,0:T(8,128)} %get-tuple-element.1730, pred[3,2048]{1,0:T(4,128)(4,1)S(1)} %broadcast_compare_fusion.38, pred[3,512]{1,0:T(4,128)(4,1)S(1)} %broadcast_compare_fusion.39, ...), kind=kLoop, calls=%fused_computation.388.clone.1 | loop fusion | flops 72350208 | bytes 27305984 | tf_op jit(solution)/shard_map/while/body/eval_jaxpr/reduce_sum | solution.py:72
  196.4 6.0 all-reduce.3
  204.9 8.7 %all_gather.21 = bf16[512,768]{0,1:T(8,128)(2,1)S(1)} all-gather(bf16[512,192]{0,1:T(8,128)(2,1)} %param.42), channel_id=1, replica_groups=mesh['seq'=8,'head'=4] {'head'}, dimensions={1}, use_global_device_ids=true | all-gather | bytes 983040 | tf_op jit(solution)/shard_map/all_gather | solution.py:178
  213.6 11.9 %reduce-scatter.4.cloned.1.call-done = bf16[512,192]{0,1:T(8,128)(2,1)} async-done(((bf16[512,768]{0,1:T(8,128)(2,1)}), bf16[512,192]{0,1:T(8,128)(2,1)}) %reduce-scatter.4.cloned.1.call-update) | async-done | bytes 196624 | tf_op jit(solution)/shard_map/reduce_scatter | solution.py:156
  226.7 8.7 %all_gather.20 = bf16[512,768]{0,1:T(8,128)(2,1)S(1)} all-gather(bf16[512,192]{0,1:T(8,128)(2,1)S(1)} %fusion.114), channel_id=1, replica_groups=mesh['seq'=8,'head'=4] {'head'}, dimensions={1}, use_global_device_ids=true | all-gather | bytes 983040 | tf_op jit(solution)/shard_map/all_gather | solution.py:164
  246.1 34.5 %all-reduce.8.cloned.1.call-done = bf16[512,768]{0,1:T(8,128)(2,1)} async-done(((bf16[512,768]{0,1:T(8,128)(2,1)}), bf16[512,768]{0,1:T(8,128)(2,1)}) %all-reduce.8.cloned.1.call-update) | async-done | bytes 786448 | tf_op jit(solution)/shard_map/psum | solution.py:187
  289.1 6.5 all-reduce.2
  298.0 104.5 %while.43 = (s32[]{:T(128)}, f32[3,512,64]{1,2,0:T(8,128)S(1)}, f32[2,2048,384]{2,1,0:T(8,128)}, s32[512]{0:T(512)S(1)}, s32[2]{0:T(128)}, /*index=5*/s32[6,1]{0...) while((s32[]{:T(128)}, f32[3,512,64]{1,2,0:T(8,128)S(1)}, ...), condition=%wide.region_30.31_spmd.clone.clone.clone, body=%wide.region_27.30_spmd.clone.clone.clone.sunk | while | flops 2108366976 | bytes 175255120 | solution.py:274
  309.0 12.4 %fusion.216 = f32[3,512,2048]{1,2,0:T(8,128)S(1)} fusion(f32[3,512]{1,0:T(4,128)S(1)} %copy-done.86, f32[512,2048]{0,1:T(8,128)S(1)} %get-tuple-element.1766, pred[3,2048]{1,0:T(4,128)(4,1)S(1)} %broadcast_compare_fusion.46, pred[3,512]{1,0:T(4,128)(4,1)S(1)} %broadcast_compare_fusion.47, pred[512,2048]{0,1:T(8,128)(4,1)S(1)} %get-tuple-element.1771, ...), kind=kOutput, calls=%fused_computation.139.clone.1 | convolution fusion | flops 468713472 | bytes 22003716 | tf_op jit(solution)/shard_map/while/body/eval_jaxpr/hqd,khd->hqk/dot_general | solution.py:227
  332.3 6.7 fusion.218
  361.2 12.4 %fusion.216 = f32[3,512,2048]{1,2,0:T(8,128)S(1)} fusion(f32[3,512]{1,0:T(4,128)S(1)} %copy-done.86, f32[512,2048]{0,1:T(8,128)S(1)} %get-tuple-element.1766, pred[3,2048]{1,0:T(4,128)(4,1)S(1)} %broadcast_compare_fusion.46, pred[3,512]{1,0:T(4,128)(4,1)S(1)} %broadcast_compare_fusion.47, pred[512,2048]{0,1:T(8,128)(4,1)S(1)} %get-tuple-element.1771, ...), kind=kOutput, calls=%fused_computation.139.clone.1 | convolution fusion | flops 468713472 | bytes 22003716 | tf_op jit(solution)/shard_map/while/body/eval_jaxpr/hqd,khd->hqk/dot_general | solution.py:227
  384.5 6.7 fusion.218
  417.4 103.4 %reduce-scatter.8.cloned.1.call-done = f32[512,384]{1,0:T(8,128)} async-done(((f32[4096,384]{1,0:T(8,128)}), f32[512,384]{1,0:T(8,128)}) %reduce-scatter.8.cloned.1.call-update) | async-done | bytes 786448 | tf_op jit(solution)/shard_map/reduce_scatter | solution.py:276
  531.6 14.2 %reduce-scatter.6.cloned.1.call-done = bf16[512,192]{0,1:T(8,128)(2,1)} async-done(((bf16[512,768]{0,1:T(8,128)(2,1)}), bf16[512,192]{0,1:T(8,128)(2,1)}) %reduce-scatter.6.cloned.1.call-update) | async-done | bytes 196624 | tf_op jit(solution)/shard_map/reduce_scatter | solution.py:170
  549.4 33.4 %all-reduce.10.cloned.1.call-done = bf16[512,768]{0,1:T(8,128)(2,1)} async-done(((bf16[512,768]{0,1:T(8,128)(2,1)}), bf16[512,768]{0,1:T(8,128)(2,1)}) %all-reduce.10.cloned.1.call-update) | async-done | bytes 786448 | tf_op jit(solution)/shard_map/psum | solution.py:291
  585.3 40.1 %all-reduce = (f32[768]{0:T(1024)}, f32[768]{0:T(1024)}, f32[192]{0:T(256)}, f32[192]{0:T(256)}, f32[192]{0:T(256)}, /*index=5*/f32[192]{0:T(256)}, f32[768]{0:T...) all-reduce(f32[768]{0:T(1024)} %get-tuple-element.1251, ...), channel_id=1, replica_groups=mesh['seq'=8,'head'=4] {'seq'}, use_global_device_ids=true, to_apply=%region_36.37 | all-reduce | flops 6144 | bytes 49152 | tf_op jit(solution)/shard_map/psum | solution.py:296
  628.6 198.8 %all-reduce.12.cloned.1.call-done = (f32[768,192]{0,1:T(8,128)}, f32[768,192]{0,1:T(8,128)}, f32[768,192]{0,1:T(8,128)}, f32[192,768]{1,0:T(8,128)}, f32[768,768]{1,0:T(8,128)}, /*index=5*/f32[768,768]{1,0:T(8,128)}) async-done(((f32[768,192]{0,1:T(8,128)}, f32[768,192]{0,1:T(8,128)}, f32[768,192]{0,1:T(8,128)}, f32[192,768]{1,0:T(8,128)}, f32[768,768]{1,0:T(8,128)}, /*index=5*/f32[768,768]{1,0:T(8,128)}), ...) | async-done | bytes 7077904 | tf_op jit(solution)/shard_map/psum | solution.py:296
  (453 shorter events, 168.9 us)
Async XLA Ops:
  7.2 229.8 %copy-start = (bf16[768,768]{1,0:T(8,128)(2,1)S(1)}, bf16[768,768]{1,0:T(8,128)(2,1)}, u32[]{:S(2)}) copy-start(bf16[768,768]{1,0:T(8,128)(2,1)} %param.40) | copy-start | bytes 3538948
  7.2 59.4 %all-gather.3.cloned.1.call-start = ((), (), s32[]{:S(2)}) async-start(), calls=%async_computation.3 | async-start | bytes 1769472 | tf_op jit(solution)/shard_map/all_gather | solution.py:136
  20.3 92.5 %all-gather.5.cloned.1.call-start = ((), (), s32[]{:S(2)}) async-start(), calls=%async_computation.4 | async-start | bytes 1769472 | tf_op jit(solution)/shard_map/all_gather | solution.py:137
  21.4 204.1 %reduce-scatter.4.cloned.1.call-start = ((), (), s32[]{:S(2)}) async-start(), calls=%async_computation.5 | async-start | bytes 983040 | tf_op jit(solution)/shard_map/reduce_scatter | solution.py:156
  202.6 22.9 %copy-start.32 = (bf16[512,192]{0,1:T(8,128)(2,1)S(1)}, bf16[512,192]{0,1:T(8,128)(2,1)}, u32[]{:S(2)}) copy-start(bf16[512,192]{0,1:T(8,128)(2,1)} %param.24) | copy-start | bytes 589828
  204.0 76.6 %all-reduce.8.cloned.1.call-start = ((), (), s32[]{:S(2)}) async-start(), calls=%async_computation.7 | async-start | bytes 1572864 | tf_op jit(solution)/shard_map/psum | solution.py:187
  204.9 30.6 %copy-start.85 = (f32[192]{0:T(256)}, f32[192]{0:T(256)S(1)}, u32[]{:S(2)}) copy-start(f32[192]{0:T(256)S(1)} %dynamic_slice.65) | copy-start | bytes 2308
  213.5 23.4 %copy-start.23 = (bf16[512,768]{0,1:T(8,128)(2,1)}, bf16[512,768]{0,1:T(8,128)(2,1)S(1)}, u32[]{:S(2)}) copy-start(bf16[512,768]{0,1:T(8,128)(2,1)S(1)} %all_gather.21) | copy-start | bytes 2359300
  213.5 22.2 %copy-start.67 = (f32[768]{0:T(1024)S(1)}, f32[768]{0:T(1024)}, u32[]{:S(2)}) copy-start(f32[768]{0:T(1024)} %param.36) | copy-start | bytes 9220
  213.6 22.2 %copy-start.93 = (f32[768]{0:T(1024)S(1)}, f32[768]{0:T(1024)}, u32[]{:S(2)}) copy-start(f32[768]{0:T(1024)} %param.39) | copy-start | bytes 9220
  213.6 22.2 %copy-start.94 = (f32[768]{0:T(1024)S(1)}, f32[768]{0:T(1024)}, u32[]{:S(2)}) copy-start(f32[768]{0:T(1024)} %param.37) | copy-start | bytes 9220
  235.3 49.3 %copy-start.9 = (bf16[512,768]{0,1:T(8,128)(2,1)}, bf16[512,768]{0,1:T(8,128)(2,1)S(1)}, u32[]{:S(2)}) copy-start(bf16[512,768]{0,1:T(8,128)(2,1)S(1)} %all_gather.20) | copy-start | bytes 2359300
  235.5 49.1 %copy-start.65 = (f32[512]{0:T(512)}, f32[512]{0:T(512)S(1)}, u32[]{:S(2)}) copy-start(f32[512]{0:T(512)S(1)} %broadcast_multiply_fusion.1) | copy-start | bytes 6148
  235.8 48.8 %copy-start.74 = (f32[512]{0:T(512)}, f32[512]{0:T(512)S(1)}, u32[]{:S(2)}) copy-start(f32[512]{0:T(512)S(1)} %fusion.123) | copy-start | bytes 6148
  243.7 36.9 %copy-start.68 = (f32[768]{0:T(1024)S(1)}, f32[768]{0:T(1024)}, u32[]{:S(2)}) copy-start(f32[768]{0:T(1024)} %param.36) | copy-start | bytes 9220
  245.5 275.3 %reduce-scatter.8.cloned.1.call-start = ((), (), s32[]{:S(2)}) async-start(), calls=%async_computation.8 | async-start | bytes 7077888 | tf_op jit(solution)/shard_map/reduce_scatter | solution.py:276
  402.5 143.2 %reduce-scatter.6.cloned.1.call-start = ((), (), s32[]{:S(2)}) async-start(), calls=%async_computation.6 | async-start | bytes 983040 | tf_op jit(solution)/shard_map/reduce_scatter | solution.py:170
  411.2 171.6 %all-reduce.10.cloned.1.call-start = ((), (), s32[]{:S(2)}) async-start(), calls=%async_computation.9 | async-start | bytes 1572864 | tf_op jit(solution)/shard_map/psum | solution.py:291
  525.1 302.3 %all-reduce.12.cloned.1.call-start = ((), (), s32[]{:S(2)}) async-start(), calls=%async_computation.10 | async-start | bytes 14155776 | tf_op jit(solution)/shard_map/psum | solution.py:296
  528.8 54.0 %copy-start.64 = (f32[512]{0:T(512)S(1)}, f32[512]{0:T(512)}, u32[]{:S(2)}) copy-start(f32[512]{0:T(512)} %copy-done.63) | copy-start | bytes 6148
  528.8 54.0 %copy-start.71 = (f32[768]{0:T(1024)S(1)}, f32[768]{0:T(1024)}, u32[]{:S(2)}) copy-start(f32[768]{0:T(1024)} %param.25) | copy-start | bytes 9220
  528.8 54.0 %copy-start.73 = (f32[512]{0:T(512)S(1)}, f32[512]{0:T(512)}, u32[]{:S(2)}) copy-start(f32[512]{0:T(512)} %copy-done.72) | copy-start | bytes 6148
  528.8 54.0 %copy-start.12 = (bf16[512,768]{0,1:T(8,128)(2,1)S(1)}, bf16[512,768]{0,1:T(8,128)(2,1)}, u32[]{:S(2)}) copy-start(bf16[512,768]{0,1:T(8,128)(2,1)} %copy-done.11) | copy-start | bytes 2359300
  528.8 96.6 %copy-start.81 = (f32[512]{0:T(512)S(1)}, f32[512]{0:T(512)}, u32[]{:S(2)}) copy-start(f32[512]{0:T(512)} %copy-done.80) | copy-start | bytes 6148
  (111 other events, 622.1 us)
Sparse Core Ops, SparseCore 0:
  20.4 46.1 all-gather.2
  69.2 43.4 all-gather.4
  204.2 21.3 reduce-scatter.3
  245.6 34.9 all-reduce.7
  402.6 118.0 reduce-scatter.7
  523.3 22.3 reduce-scatter.5
  548.1 34.6 all-reduce.9
  589.6 237.7 all-reduce.11
where the time goes:
time: 852 us; the launch traced here: 843 us
  waiting for transfers between devices  482 us (57%)
  matrix products  120 us (14%)
  other arithmetic  95.7 us (11%)
  blocking collectives  80.4 us (9%)
  local copies, waits for them, and re-layouts  48.5 us (6%)
  between operations  15.1 us (2%)
    psum x1, waiting for transfers between devices, shards(): lax.psum((grad_ln1_gain, grad_ln1_bias, grad_w_query, grad_b_query, grad_...  199 us
    reduce_scatter x1, waiting for transfers between devices, shards(): lax.psum_scatter(key_terms, 'seq', scatter_dimension=0, tiled=True)  103 us
    all_gather x1, waiting for transfers between devices, shards(): lax.all_gather(key_rows, 'seq', axis=0, tiled=True)  43.9 us
    all_gather x1, waiting for transfers between devices, shards(): lax.all_gather(values, 'seq', axis=0, tiled=True)  41.5 us
    psum x1, blocking collectives, shards(): lax.psum((grad_ln1_gain, grad_ln1_bias, grad_w_query, grad_b_query, grad_...  40.1 us
    psum x1, waiting for transfers between devices, shards(): lax.psum(jnp.dot(grad_inner, w_up.T, preferred_element_type=jnp.float32)....  34.5 us
    psum x1, waiting for transfers between devices, shards(): lax.psum(grad_normed.astype(jnp.bfloat16), 'head').astype(jnp.float32)  33.4 us
    reduce_sum x2, other arithmetic, advance(): totals = totals * factor + jnp.sum(weights, axis=-1)  33.3 us
  transfers between devices with their start and end apart: 8, of which 8 were waited for; matrix products, arithmetic and copies ran while one was open for 5% of the time, Pallas kernels for 0%

commit v1 on v0

--- a/solution.py
+++ b/solution.py
@@ -9,6 +9,35 @@
 eps = 1e-05
 segment_scales = (1, 2, 4, 8, 16)
 dilation_steps = (1, 2, 4, 6, 12)
+
+
+def see_the_floor(panel):
+    current_arr = lax.axis_size("seq")
+    y = lax.axis_index("seq")
+    work_now, u1, out_arr = (current_arr, y, panel.shape[0])
+    outcome_arr = jnp.zeros(
+        [dev * work_now if hop_no == 0 else dev for hop_no, dev in enumerate(panel.shape)],
+        panel.dtype,
+    )
+    part_now = lax.dynamic_update_slice_in_dim(outcome_arr, panel, u1 * out_arr, axis=0)
+    w1 = back = panel
+    for tick in tuple(range(1, work_now // 2 + 1)):
+        w1 = lax.ppermute(
+            w1,
+            axis_name="seq",
+            perm=[(hop_no, (hop_no + 1) % work_now) for hop_no in range(work_now)],
+        )
+        part_now = lax.dynamic_update_slice_in_dim(
+            part_now, w1, (u1 - tick) % work_now * out_arr, axis=0
+        )
+        if 2 * tick < work_now:
+            back = lax.ppermute(
+                back, "seq", [(hop_no, (hop_no - 1) % work_now) for hop_no in range(work_now)]
+            )
+            part_now = lax.dynamic_update_slice_in_dim(
+                part_now, back, (u1 + tick) % work_now * out_arr, axis=0
+            )
+    return part_now
 
 
 def layer_norm(inputs, norm_gain, norm_bias):
@@ -132,10 +161,7 @@
     )
     highest, totals, running_sum = fold_keys(
         start_state,
-        (
-            lax.all_gather(key_rows, "seq", axis=0, tiled=True),
-            lax.all_gather(values, "seq", axis=0, tiled=True),
-        ),
+        (lax.all_gather(key_rows, "seq", axis=0, tiled=True), see_the_floor(values)),
         query_heads,
         head_ids,
         query_row,

time: 852 us -> 844 us (level)
  waiting for transfers between devices: 482 us -> 445 us
  starting transfers between devices: 0.54 us -> 18 us
  local copies, waits for them, and re-layouts: 48.5 us -> 60.5 us
    all_gather x1, waiting for transfers between devices: 43.9 us -> 0.83 us  [shards(): lax.all_gather(key_rows, 'seq', axis=0, tiled=True)]
    ppermute x0 -> x7, waiting for transfers between devices: none -> 25.2 us  [the longest x4 25.2 us: see_the_floor(): lax.ppermute(w1, axis_name='seq', perm=[(hop_no, (hop_no + 1) % work_now)...]
    ppermute x0 -> x7, starting transfers between devices: none -> 17.4 us  [the longest x3 9.17 us: see_the_floor(): lax.ppermute(back, 'seq', [(hop_no, (hop_no - 1) % work_now) for hop_no i...]
    all_gather x1, waiting for transfers between devices: 41.5 us -> 28.7 us  [shards(): lax.all_gather(values, 'seq', axis=0, tiled=True)]
    unnamed x158 -> x163, local copies, waits for them, and re-layouts: 15.4 us -> 18.8 us
  transfers between devices with their start and end apart: 8 -> 15, of which waited for: 8 -> 12; matrix products, arithmetic and copies ran while one was open for 5% -> 8% of each run, Pallas kernels for 0% -> 0%
where the time goes in v1:
time: 844 us; the launch traced here: 834 us
  waiting for transfers between devices  445 us (53%)
  matrix products  120 us (14%)
  other arithmetic  95.3 us (11%)
  blocking collectives  80 us (9%)
  local copies, waits for them, and re-layouts  60.5 us (7%)
  starting transfers between devices  18 us (2%)
  between operations  15.1 us (2%)
    psum x1, waiting for transfers between devices, shards(): lax.psum((grad_ln1_gain, grad_ln1_bias, grad_w_query, grad_b_query, grad_...  199 us
    reduce_scatter x1, waiting for transfers between devices, shards(): lax.psum_scatter(key_terms, 'seq', scatter_dimension=0, tiled=True)  103 us
    psum x1, blocking collectives, shards(): lax.psum((grad_ln1_gain, grad_ln1_bias, grad_w_query, grad_b_query, grad_...  40.1 us
    psum x1, waiting for transfers between devices, shards(): lax.psum(grad_normed.astype(jnp.bfloat16), 'head').astype(jnp.float32)  33.3 us
    reduce_sum x2, other arithmetic, advance(): totals = totals * factor + jnp.sum(weights, axis=-1)  33.3 us
    all_gather x1, waiting for transfers between devices, shards(): lax.all_gather(values, 'seq', axis=0, tiled=True)  28.7 us
    psum x1, waiting for transfers between devices, shards(): lax.psum(jnp.dot(grad_inner, w_up.T, preferred_element_type=jnp.float32)....  27.4 us
    ppermute x4, waiting for transfers between devices, see_the_floor(): lax.ppermute(w1, axis_name='seq', perm=[(hop_no, (hop_no + 1) % work_now)...  25.2 us
  transfers between devices with their start and end apart: 15, of which 12 were waited for; matrix products, arithmetic and copies ran while one was open for 8% of the time, Pallas kernels for 0%

profile of v1, /device:TPU:0, one launch (start us, length us, event | category | flops | bytes accessed | tf_op | source)
XLA Modules:
  0.0 834.3 jit_solution(186150525657373623)
XLA Ops:
  7.3 10.4 %all_gather.16 = bf16[512,768]{0,1:T(8,128)(2,1)S(1)} all-gather(bf16[512,192]{0,1:T(8,128)(2,1)} %param.24), channel_id=1, replica_groups=mesh['seq'=8,'head'=4] {'head'}, dimensions={1}, use_global_device_ids=true | all-gather | bytes 983040 | tf_op jit(solution)/shard_map/all_gather | solution.py:147
  28.2 7.0 collective-permute-done
  52.8 7.7 collective-permute-done.4
  81.1 76.5 %while.42 = (s32[]{:T(128)}, f32[3,512]{1,0:T(4,128)S(1)}, f32[3,512]{1,0:T(4,128)}, f32[3,512,64]{1,2,0:T(8,128)}, s32[512]{0:T(512)S(1)}, /*index=5*/s32[2]{0:...) while((s32[]{:T(128)}, f32[3,512]{1,0:T(4,128)S(1)}, ...), condition=%wide.region_10.11_spmd.clone.clone.clone, body=%wide.region_5.10_spmd.clone.clone.clone.sunk | while | flops 955956864 | bytes 106965504 | solution.py:110
  88.3 12.1 %fusion.202 = (f32[3,512]{1,0:T(4,128)S(1)}, f32[3,2048,512]{2,1,0:T(8,128)}) fusion(f32[512,2048]{0,1:T(8,128)S(1)} %get-tuple-element.1713, pred[3,2048]{1,0:T(4,128)(4,1)S(1)} %broadcast_compare_fusion.38, pred[3,512]{1,0:T(4,128)(4,1)S(1)} %broadcast_compare_fusion.39, pred[512,2048]{0,1:T(8,128)(4,1)S(1)} %get-tuple-element.1718, ...), kind=kOutput, calls=%fused_computation.7.clone.1 | convolution fusion | flops 465566208 | bytes 22001668 | tf_op jit(solution)/shard_map/while/body/eval_jaxpr/hqd,khd->hqk/dot_general | solution.py:94
  100.5 16.7 %fusion.203 = (f32[3,512]{1,0:T(4,128)S(1)}, bf16[3,512,2048]{1,2,0:T(8,128)(2,1)S(1)}) fusion(f32[3,512]{1,0:T(4,128)S(1)} %select_maximum_fusion.2, f32[3,2048,512]{2,1,0:T(8,128)} %get-tuple-element.1732, pred[3,2048]{1,0:T(4,128)(4,1)S(1)} %broadcast_compare_fusion.38, pred[3,512]{1,0:T(4,128)(4,1)S(1)} %broadcast_compare_fusion.39, ...), kind=kLoop, calls=%fused_computation.396.clone.1 | loop fusion | flops 72350208 | bytes 27305984 | tf_op jit(solution)/shard_map/while/body/eval_jaxpr/reduce_sum | solution.py:101
  126.6 12.1 %fusion.202 = (f32[3,512]{1,0:T(4,128)S(1)}, f32[3,2048,512]{2,1,0:T(8,128)}) fusion(f32[512,2048]{0,1:T(8,128)S(1)} %get-tuple-element.1713, pred[3,2048]{1,0:T(4,128)(4,1)S(1)} %broadcast_compare_fusion.38, pred[3,512]{1,0:T(4,128)(4,1)S(1)} %broadcast_compare_fusion.39, pred[512,2048]{0,1:T(8,128)(4,1)S(1)} %get-tuple-element.1718, ...), kind=kOutput, calls=%fused_computation.7.clone.1 | convolution fusion | flops 465566208 | bytes 22001668 | tf_op jit(solution)/shard_map/while/body/eval_jaxpr/hqd,khd->hqk/dot_general | solution.py:94
  138.8 16.7 %fusion.203 = (f32[3,512]{1,0:T(4,128)S(1)}, bf16[3,512,2048]{1,2,0:T(8,128)(2,1)S(1)}) fusion(f32[3,512]{1,0:T(4,128)S(1)} %select_maximum_fusion.2, f32[3,2048,512]{2,1,0:T(8,128)} %get-tuple-element.1732, pred[3,2048]{1,0:T(4,128)(4,1)S(1)} %broadcast_compare_fusion.38, pred[3,512]{1,0:T(4,128)(4,1)S(1)} %broadcast_compare_fusion.39, ...), kind=kLoop, calls=%fused_computation.396.clone.1 | loop fusion | flops 72350208 | bytes 27305984 | tf_op jit(solution)/shard_map/while/body/eval_jaxpr/reduce_sum | solution.py:101
  167.6 8.5 %all_gather.19 = bf16[512,768]{0,1:T(8,128)(2,1)S(1)} all-gather(bf16[512,192]{0,1:T(8,128)(2,1)} %param.42), channel_id=1, replica_groups=mesh['seq'=8,'head'=4] {'head'}, dimensions={1}, use_global_device_ids=true | all-gather | bytes 983040 | tf_op jit(solution)/shard_map/all_gather | solution.py:204
  176.9 11.9 %reduce-scatter.4.cloned.1.call-done = bf16[512,192]{0,1:T(8,128)(2,1)} async-done(((bf16[512,768]{0,1:T(8,128)(2,1)}), bf16[512,192]{0,1:T(8,128)(2,1)}) %reduce-scatter.4.cloned.1.call-update) | async-done | bytes 196624 | tf_op jit(solution)/shard_map/reduce_scatter | solution.py:182
  190.0 8.2 all_gather.18
  208.3 28.7 %all-gather.5.cloned.1.call-done = bf16[4096,192]{0,1:T(8,128)(2,1)} async-done(((bf16[512,192]{0,1:T(8,128)(2,1)}), bf16[4096,192]{0,1:T(8,128)(2,1)}) %all-gather.5.cloned.1.call-update) | async-done | bytes 1572880 | tf_op jit(solution)/shard_map/all_gather | solution.py:240
  244.8 27.4 %all-reduce.8.cloned.1.call-done = bf16[512,768]{0,1:T(8,128)(2,1)} async-done(((bf16[512,768]{0,1:T(8,128)(2,1)}), bf16[512,768]{0,1:T(8,128)(2,1)}) %all-reduce.8.cloned.1.call-update) | async-done | bytes 786448 | tf_op jit(solution)/shard_map/psum | solution.py:213
  280.7 6.5 all-reduce.2
  289.6 104.3 %while.43 = (s32[]{:T(128)}, f32[3,512,64]{1,2,0:T(8,128)S(1)}, f32[2,2048,384]{2,1,0:T(8,128)}, s32[512]{0:T(512)S(1)}, s32[2]{0:T(128)}, /*index=5*/s32[6,1]{0...) while((s32[]{:T(128)}, f32[3,512,64]{1,2,0:T(8,128)S(1)}, ...), condition=%wide.region_30.31_spmd.clone.clone.clone, body=%wide.region_27.30_spmd.clone.clone.clone.sunk | while | flops 2108366976 | bytes 175255120 | solution.py:300
  300.6 12.5 %fusion.216 = f32[3,512,2048]{1,2,0:T(8,128)S(1)} fusion(f32[3,512]{1,0:T(4,128)S(1)} %copy-done.87, f32[512,2048]{0,1:T(8,128)S(1)} %get-tuple-element.1768, pred[3,2048]{1,0:T(4,128)(4,1)S(1)} %broadcast_compare_fusion.46, pred[3,512]{1,0:T(4,128)(4,1)S(1)} %broadcast_compare_fusion.47, pred[512,2048]{0,1:T(8,128)(4,1)S(1)} %get-tuple-element.1773, ...), kind=kOutput, calls=%fused_computation.139.clone.1 | convolution fusion | flops 468713472 | bytes 22003716 | tf_op jit(solution)/shard_map/while/body/eval_jaxpr/hqd,khd->hqk/dot_general | solution.py:253
  323.8 6.7 fusion.218
  352.8 12.5 %fusion.216 = f32[3,512,2048]{1,2,0:T(8,128)S(1)} fusion(f32[3,512]{1,0:T(4,128)S(1)} %copy-done.87, f32[512,2048]{0,1:T(8,128)S(1)} %get-tuple-element.1768, pred[3,2048]{1,0:T(4,128)(4,1)S(1)} %broadcast_compare_fusion.46, pred[3,512]{1,0:T(4,128)(4,1)S(1)} %broadcast_compare_fusion.47, pred[512,2048]{0,1:T(8,128)(4,1)S(1)} %get-tuple-element.1773, ...), kind=kOutput, calls=%fused_computation.139.clone.1 | convolution fusion | flops 468713472 | bytes 22003716 | tf_op jit(solution)/shard_map/while/body/eval_jaxpr/hqd,khd->hqk/dot_general | solution.py:253
  375.9 6.7 fusion.218
  408.8 103.4 %reduce-scatter.8.cloned.1.call-done = f32[512,384]{1,0:T(8,128)} async-done(((f32[4096,384]{1,0:T(8,128)}), f32[512,384]{1,0:T(8,128)}) %reduce-scatter.8.cloned.1.call-update) | async-done | bytes 786448 | tf_op jit(solution)/shard_map/reduce_scatter | solution.py:302
  523.0 14.2 %reduce-scatter.6.cloned.1.call-done = bf16[512,192]{0,1:T(8,128)(2,1)} async-done(((bf16[512,768]{0,1:T(8,128)(2,1)}), bf16[512,192]{0,1:T(8,128)(2,1)}) %reduce-scatter.6.cloned.1.call-update) | async-done | bytes 196624 | tf_op jit(solution)/shard_map/reduce_scatter | solution.py:196
  540.9 33.3 %all-reduce.10.cloned.1.call-done = bf16[512,768]{0,1:T(8,128)(2,1)} async-done(((bf16[512,768]{0,1:T(8,128)(2,1)}), bf16[512,768]{0,1:T(8,128)(2,1)}) %all-reduce.10.cloned.1.call-update) | async-done | bytes 786448 | tf_op jit(solution)/shard_map/psum | solution.py:317
  576.7 40.1 %all-reduce = (f32[768]{0:T(1024)}, f32[768]{0:T(1024)}, f32[192]{0:T(256)}, f32[192]{0:T(256)}, f32[192]{0:T(256)}, /*index=5*/f32[192]{0:T(256)}, f32[768]{0:T...) all-reduce(f32[768]{0:T(1024)} %get-tuple-element.1251, ...), channel_id=1, replica_groups=mesh['seq'=8,'head'=4] {'seq'}, use_global_device_ids=true, to_apply=%region_36.37 | all-reduce | flops 6144 | bytes 49152 | tf_op jit(solution)/shard_map/psum | solution.py:322
  620.0 198.8 %all-reduce.12.cloned.1.call-done = (f32[768,192]{0,1:T(8,128)}, f32[768,192]{0,1:T(8,128)}, f32[768,192]{0,1:T(8,128)}, f32[192,768]{1,0:T(8,128)}, f32[768,768]{1,0:T(8,128)}, /*index=5*/f32[768,768]{1,0:T(8,128)}) async-done(((f32[768,192]{0,1:T(8,128)}, f32[768,192]{0,1:T(8,128)}, f32[768,192]{0,1:T(8,128)}, f32[192,768]{1,0:T(8,128)}, f32[768,768]{1,0:T(8,128)}, /*index=5*/f32[768,768]{1,0:T(8,128)}), ...) | async-done | bytes 7077904 | tf_op jit(solution)/shard_map/psum | solution.py:322
  (489 shorter events, 216.1 us)
Async XLA Ops:
  7.2 192.6 %copy-start = (bf16[768,768]{1,0:T(8,128)(2,1)S(1)}, bf16[768,768]{1,0:T(8,128)(2,1)}, u32[]{:S(2)}) copy-start(bf16[768,768]{1,0:T(8,128)(2,1)} %param.40) | copy-start | bytes 3538948
  7.2 69.3 %all-gather.3.cloned.1.call-start = ((), (), s32[]{:S(2)}) async-start(), calls=%async_computation.3 | async-start | bytes 1769472 | tf_op jit(solution)/shard_map/all_gather | solution.py:164
  20.3 168.5 %reduce-scatter.4.cloned.1.call-start = ((), (), s32[]{:S(2)}) async-start(), calls=%async_computation.4 | async-start | bytes 983040 | tf_op jit(solution)/shard_map/reduce_scatter | solution.py:182
  22.7 12.5 %collective-permute-start = (bf16[512,192]{0,1:T(8,128)(2,1)S(1)}, bf16[512,192]{0,1:T(8,128)(2,1)S(1)}, u32[]{:S(2)}, u32[]{:S(2)}) collective-permute-start(bf16[512,192]{0,1:T(8,128)(2,1)S(1)} %get-tuple-element.1440), channel_id=1, source_target_pairs={{0,4},{4,8},{8,12},{12,16},{16,20},{20,24},{24,28},{28,0},{1,5},{5... | collective-permute-start | bytes 589832 | tf_op jit(solution)/shard_map/ppermute | solution.py:25
  24.3 13.5 %collective-permute-start.1 = (bf16[512,192]{0,1:T(8,128)(2,1)S(1)}, bf16[512,192]{0,1:T(8,128)(2,1)S(1)}, u32[]{:S(2)}, u32[]{:S(2)}) collective-permute-start(bf16[512,192]{0,1:T(8,128)(2,1)S(1)} %get-tuple-element.1440), channel_id=1, source_target_pairs={{0,28},{4,0},{8,4},{12,8},{16,12},{20,16},{24,20},{28,24},{1,29},{... | collective-permute-start | bytes 589832 | tf_op jit(solution)/shard_map/ppermute | solution.py:34
  35.3 11.2 %collective-permute-start.2 = (bf16[512,192]{0,1:T(8,128)(2,1)S(1)}, bf16[512,192]{0,1:T(8,128)(2,1)S(1)}, u32[]{:S(2)}, u32[]{:S(2)}) collective-permute-start(bf16[512,192]{0,1:T(8,128)(2,1)S(1)} %collective-permute-done), channel_id=1, source_target_pairs={{0,4},{4,8},{8,12},{12,16},{16,20},{20,24},{24,28},{28,0},{1,5},{5... | collective-permute-start | bytes 589832 | tf_op jit(solution)/shard_map/ppermute | solution.py:25
  37.7 10.5 %collective-permute-start.3 = (bf16[512,192]{0,1:T(8,128)(2,1)S(1)}, bf16[512,192]{0,1:T(8,128)(2,1)S(1)}, u32[]{:S(2)}, u32[]{:S(2)}) collective-permute-start(bf16[512,192]{0,1:T(8,128)(2,1)S(1)} %collective-permute-done.1), channel_id=1, source_target_pairs={{0,28},{4,0},{8,4},{12,8},{16,12},{20,16},{24,20},{28,24},{1,29},{... | collective-permute-start | bytes 589832 | tf_op jit(solution)/shard_map/ppermute | solution.py:34
  46.4 14.1 %collective-permute-start.4 = (bf16[512,192]{0,1:T(8,128)(2,1)S(1)}, bf16[512,192]{0,1:T(8,128)(2,1)S(1)}, u32[]{:S(2)}, u32[]{:S(2)}) collective-permute-start(bf16[512,192]{0,1:T(8,128)(2,1)S(1)} %collective-permute-done.2), channel_id=1, source_target_pairs={{0,4},{4,8},{8,12},{12,16},{16,20},{20,24},{24,28},{28,0},{1,5},{5... | collective-permute-start | bytes 589832 | tf_op jit(solution)/shard_map/ppermute | solution.py:25
  48.2 15.4 %collective-permute-start.5 = (bf16[512,192]{0,1:T(8,128)(2,1)S(1)}, bf16[512,192]{0,1:T(8,128)(2,1)S(1)}, u32[]{:S(2)}, u32[]{:S(2)}) collective-permute-start(bf16[512,192]{0,1:T(8,128)(2,1)S(1)} %collective-permute-done.3), channel_id=1, source_target_pairs={{0,28},{4,0},{8,4},{12,8},{16,12},{20,16},{24,20},{28,24},{1,29},{... | collective-permute-start | bytes 589832 | tf_op jit(solution)/shard_map/ppermute | solution.py:34
  60.5 9.9 %collective-permute-start.6 = (bf16[512,192]{0,1:T(8,128)(2,1)S(1)}, bf16[512,192]{0,1:T(8,128)(2,1)S(1)}, u32[]{:S(2)}, u32[]{:S(2)}) collective-permute-start(bf16[512,192]{0,1:T(8,128)(2,1)S(1)} %collective-permute-done.4), channel_id=1, source_target_pairs={{0,4},{4,8},{8,12},{12,16},{16,20},{20,24},{24,28},{28,0},{1,5},{5... | collective-permute-start | bytes 589832 | tf_op jit(solution)/shard_map/ppermute | solution.py:25
  166.8 70.2 %all-gather.5.cloned.1.call-start = ((), (), s32[]{:S(2)}) async-start(), calls=%async_computation.7 | async-start | bytes 1769472 | tf_op jit(solution)/shard_map/all_gather | solution.py:240
  167.6 104.6 %all-reduce.8.cloned.1.call-start = ((), (), s32[]{:S(2)}) async-start(), calls=%async_computation.6 | async-start | bytes 1572864 | tf_op jit(solution)/shard_map/psum | solution.py:213
  198.2 78.0 %copy-start.7 = (bf16[512,768]{0,1:T(8,128)(2,1)}, bf16[512,768]{0,1:T(8,128)(2,1)S(1)}, u32[]{:S(2)}) copy-start(bf16[512,768]{0,1:T(8,128)(2,1)S(1)} %all_gather.18) | copy-start | bytes 2359300
  198.4 77.8 %copy-start.66 = (f32[512]{0:T(512)}, f32[512]{0:T(512)S(1)}, u32[]{:S(2)}) copy-start(f32[512]{0:T(512)S(1)} %broadcast_multiply_fusion.1) | copy-start | bytes 6148
  198.7 77.5 %copy-start.75 = (f32[512]{0:T(512)}, f32[512]{0:T(512)S(1)}, u32[]{:S(2)}) copy-start(f32[512]{0:T(512)S(1)} %fusion.123) | copy-start | bytes 6148
  208.3 303.9 %reduce-scatter.8.cloned.1.call-start = ((), (), s32[]{:S(2)}) async-start(), calls=%async_computation.8 | async-start | bytes 7077888 | tf_op jit(solution)/shard_map/reduce_scatter | solution.py:302
  393.9 143.3 %reduce-scatter.6.cloned.1.call-start = ((), (), s32[]{:S(2)}) async-start(), calls=%async_computation.5 | async-start | bytes 983040 | tf_op jit(solution)/shard_map/reduce_scatter | solution.py:196
  402.6 171.6 %all-reduce.10.cloned.1.call-start = ((), (), s32[]{:S(2)}) async-start(), calls=%async_computation.9 | async-start | bytes 1572864 | tf_op jit(solution)/shard_map/psum | solution.py:317
  516.5 302.2 %all-reduce.12.cloned.1.call-start = ((), (), s32[]{:S(2)}) async-start(), calls=%async_computation.10 | async-start | bytes 14155776 | tf_op jit(solution)/shard_map/psum | solution.py:322
  520.3 53.9 %copy-start.65 = (f32[512]{0:T(512)S(1)}, f32[512]{0:T(512)}, u32[]{:S(2)}) copy-start(f32[512]{0:T(512)} %copy-done.64) | copy-start | bytes 6148
  520.3 53.9 %copy-start.72 = (f32[768]{0:T(1024)S(1)}, f32[768]{0:T(1024)}, u32[]{:S(2)}) copy-start(f32[768]{0:T(1024)} %param.25) | copy-start | bytes 9220
  520.3 53.9 %copy-start.74 = (f32[512]{0:T(512)S(1)}, f32[512]{0:T(512)}, u32[]{:S(2)}) copy-start(f32[512]{0:T(512)} %copy-done.73) | copy-start | bytes 6148
  520.3 53.9 %copy-start.10 = (bf16[512,768]{0,1:T(8,128)(2,1)S(1)}, bf16[512,768]{0,1:T(8,128)(2,1)}, u32[]{:S(2)}) copy-start(bf16[512,768]{0,1:T(8,128)(2,1)} %copy-done.9) | copy-start | bytes 2359300
  520.3 96.5 %copy-start.82 = (f32[512]{0:T(512)S(1)}, f32[512]{0:T(512)}, u32[]{:S(2)}) copy-start(f32[512]{0:T(512)} %copy-done.81) | copy-start | bytes 6148
  (124 other events, 852.9 us)
Sparse Core Ops, SparseCore 0:
  20.4 55.9 all-gather.2
  166.9 21.8 reduce-scatter.3
  191.6 45.3 all-gather.4
  239.4 32.7 all-reduce.7
  394.0 118.1 reduce-scatter.7
  514.7 22.4 reduce-scatter.5
  539.6 34.5 all-reduce.9
  581.0 237.7 all-reduce.11
